TPU v7x, 256 devices: a whole 4x4x8 slice. The times are simulated.
256 devices in a mesh: alpha: 8 (over x_hi, y), beta: 32 (over z, x_lo, core).
Axes of the slice: x: 4 (x_hi: 2, x_lo: 2; x = x_hi * 2 + x_lo), y: 4, z: 8, core: 2. Of those that a mesh axis runs over, the one named last changes fastest.
Arguments:
- ci_vector: float32 [7168, 28672], P('alpha', 'beta'), may hold values from -6 to 6
- diagonal: float32 [7168, 28672], P('alpha', 'beta'), may hold values from -1.5 to 1.5
- energy: float32 [1], replicated, may hold values from -0.5 to 0.5
- alpha_partner: int32 [8, 2], P('alpha'), may hold values from 0 to 7, as said below
- alpha_coupling: bfloat16 [8, 2, 896, 896], P('alpha'), may hold values from -0.1875 to 0.1875
- alpha_mask: int32 [8, 2, 7, 7], P('alpha'), may hold values 0 or 1
- beta_partner: int32 [32, 2], P('beta'), may hold values from 0 to 31, as said below
- beta_coupling: bfloat16 [32, 2, 896, 896], P('beta', None, 'alpha'), may hold values from -0.1875 to 0.1875
- beta_mask: int32 [32, 2, 7, 7], P('beta'), may hold values 0 or 1
Outputs:
- correction: float32 [7168, 28672], P('alpha', 'beta')
Inputs may be any that keep to these rules, and one draw needn't show every extreme that they name: alpha_partner[i, s] equals i with exactly one bit of its binary index flipped, and the two partners of a tile flip different bits. beta_partner[j, s] equals j with exactly one bit of its binary index flipped, and the two partners of a tile flip different bits.
All inputs are finite; a program needn't handle non-finite values. No bound on the sum of `alpha_mask` or of `beta_mask` on one device may be relied on, other than what follows from the above.
Results may differ from a plain program's by a relative error of at most 0.0003.
Values may be sent and summed in bfloat16 or wider, within the bound.
A program may use at most 128 MiB of HBM per device.

v0:
```python
import jax
import jax.numpy as jnp
from jax import lax
from jax.sharding import PartitionSpec as P

BLOCK = 128


def from_partner(value, axis, apart):
    return lax.ppermute(value, axis, [(i, i ^ 1 << apart) for i in range(lax.axis_size(axis))])


def expand_mask(block_mask):
    values = block_mask.astype(jnp.float32)
    values = jnp.repeat(values, BLOCK, axis=-2)
    return jnp.repeat(values, BLOCK, axis=-1)


def beta_part(ci_vector, beta_partner, beta_coupling, beta_mask):
    highest = lax.Precision.HIGHEST
    bit_total = lax.axis_size("beta").bit_length() - 1
    beta_index = lax.axis_index("beta")
    first_tile = jnp.zeros_like(ci_vector)
    second_tile = jnp.zeros_like(ci_vector)
    levels = list(range(bit_total))
    outgoing = ci_vector
    for level in levels:
        arrived = from_partner(outgoing, "beta", level)
        source = jnp.bitwise_xor(beta_index, 1 << level)
        first_tile = jnp.where(beta_partner[0, 0] == source, arrived, first_tile)
        second_tile = jnp.where(beta_partner[0, 1] == source, arrived, second_tile)
        outgoing = lax.optimization_barrier((outgoing, first_tile, second_tile))[0]
    full_mask = expand_mask(beta_mask[0])
    weights = (
        lax.all_gather(beta_coupling, "alpha", axis=2, tiled=True)[0].astype(jnp.float32)
        * full_mask
    )
    summed = jnp.dot(first_tile, weights[0], precision=highest)
    return summed + jnp.dot(second_tile, weights[1], precision=highest)


def alpha_part(ci_vector, alpha_partner, alpha_coupling, alpha_mask):
    highest = lax.Precision.HIGHEST
    bit_total = lax.axis_size("alpha").bit_length() - 1
    alpha_index = lax.axis_index("alpha")
    first_rows = jnp.zeros_like(ci_vector)
    second_rows = jnp.zeros_like(ci_vector)
    for level in range(bit_total):
        arrived = from_partner(ci_vector, "alpha", level)
        source = jnp.bitwise_xor(alpha_index, 1 << level)
        first_rows = jnp.where(alpha_partner[0, 0] == source, arrived, first_rows)
        second_rows = jnp.where(alpha_partner[0, 1] == source, arrived, second_rows)
    weights = alpha_coupling[0].astype(jnp.float32) * expand_mask(alpha_mask[0])
    summed = jnp.dot(weights[0].T, first_rows, precision=highest)
    return summed + jnp.dot(weights[1].T, second_rows, precision=highest)


def local(
    ci_vector,
    diagonal,
    energy,
    alpha_partner,
    alpha_coupling,
    alpha_mask,
    beta_partner,
    beta_coupling,
    beta_mask,
):
    beta_term = beta_part(ci_vector, beta_partner, beta_coupling, beta_mask)
    alpha_term = alpha_part(ci_vector, alpha_partner, alpha_coupling, alpha_mask)
    sigma = alpha_term + beta_term
    gap = diagonal - energy[0]
    return (sigma - energy[0] * ci_vector) * gap / (gap * gap + 0.0625)


def solution(mesh):
    return jax.shard_map(
        local,
        mesh=mesh,
        in_specs=(
            P("alpha", "beta"),
            P("alpha", "beta"),
            P(),
            P("alpha", None),
            P("alpha", None, None, None),
            P("alpha", None, None, None),
            P("beta", None),
            P("beta", None, "alpha", None),
            P("beta", None, None, None),
        ),
        out_specs=P("alpha", "beta"),
        check_vma=False,
    )
```

profile of v0, /device:TPU:4, one launch (start us, length us, event | category | flops | bytes accessed | tf_op | source)
XLA Modules:
  0.0 499.2 jit_solution(15112704289235251164)
XLA Ops:
  6.5 0.0 all-gather.2.cloned.1.call-start
  6.5 0.0 collective-permute-start.3
  6.5 1.3 fusion.27
  9.1 3.5 collective-permute-done.3
  12.6 4.0 broadcast_select_fusion
  16.6 1.2 collective-permute-start.4
  19.1 69.4 %collective-permute-done.4 = f32[896,896]{1,0:T(8,128)} collective-permute-done((f32[896,896]{1,0:T(8,128)}, f32[896,896]{1,0:T(8,128)}, u32[]{:S(2)}, u32[]{:S(2)}) %collective-permute-start.4) | collective-permute-done | bytes 3211296 | tf_op jit(solution)/shard_map/ppermute | solution.py:10
  88.5 6.1 %broadcast_select_fusion.6 = (f32[896,896]{1,0:T(8,128)}, f32[896,896]{1,0:T(8,128)}) fusion(f32[896,896]{1,0:T(8,128)} %collective-permute-done.4, f32[896,896]{1,0:T(8,128)S(1)} %get-tuple-element.19, pred[]{:T(512)S(6)} %eq.58, f32[896,896]{1,0:T(8,128)} %get-tuple-element.20, pred[]{:T(512)S(6)} %eq.57), kind=kLoop, calls=%fused_computation.28 | loop fusion | flops 1605632 | bytes 16056322 | tf_op jit(solution)/shard_map/jit(_where)/select_n | solution.py:31
  94.6 1.9 collective-permute-start.5
  97.8 0.0 copy-start.5
  97.8 67.9 %collective-permute-done.5 = f32[896,896]{1,0:T(8,128)S(1)} collective-permute-done((f32[896,896]{1,0:T(8,128)}, f32[896,896]{1,0:T(8,128)S(1)}, u32[]{:S(2)}, u32[]{:S(2)}) %collective-permute-start.5) | collective-permute-done | bytes 3211296 | tf_op jit(solution)/shard_map/ppermute | solution.py:10
  165.7 5.2 %broadcast_select_fusion.4 = (f32[896,896]{1,0:T(8,128)}, f32[896,896]{1,0:T(8,128)}) fusion(f32[896,896]{1,0:T(8,128)S(1)} %collective-permute-done.5, f32[896,896]{1,0:T(8,128)} %get-tuple-element.17, pred[]{:T(512)S(6)} %eq.60, f32[896,896]{1,0:T(8,128)} %get-tuple-element.18, pred[]{:T(512)S(6)} %eq.59), kind=kLoop, calls=%fused_computation.26 | loop fusion | flops 1605632 | bytes 16056322 | tf_op jit(solution)/shard_map/jit(_where)/select_n | solution.py:31
  170.9 3.3 collective-permute-start.6
  174.2 0.0 copy-done.5
  174.2 1.1 copy.25
  175.3 0.0 all-gather.2.cloned.1.call-update
  175.3 1.7 collective-permute-start.2
  177.0 2.9 collective-permute-start.1
  179.9 0.5 collective-permute-start
  181.6 0.0 copy-start.8
  181.7 0.0 copy-start.6
  181.7 0.0 copy-start.7
  181.7 130.2 %collective-permute-done.6 = f32[896,896]{1,0:T(8,128)} collective-permute-done((f32[896,896]{1,0:T(8,128)}, f32[896,896]{1,0:T(8,128)}, u32[]{:S(2)}, u32[]{:S(2)}) %collective-permute-start.6) | collective-permute-done | bytes 3211296 | tf_op jit(solution)/shard_map/ppermute | solution.py:10
  311.8 7.1 %broadcast_select_fusion.2 = (f32[896,896]{1,0:T(8,128)}, f32[896,896]{1,0:T(8,128)}) fusion(f32[896,896]{1,0:T(8,128)} %collective-permute-done.6, f32[896,896]{1,0:T(8,128)} %get-tuple-element.15, pred[]{:T(512)S(6)} %eq.62, f32[896,896]{1,0:T(8,128)} %get-tuple-element.16, pred[]{:T(512)S(6)} %eq.61), kind=kLoop, calls=%fused_computation.24 | loop fusion | flops 1605632 | bytes 16056322 | tf_op jit(solution)/shard_map/jit(_where)/select_n | solution.py:31
  318.9 5.9 %collective-permute-start.7 = (f32[896,896]{1,0:T(8,128)}, f32[896,896]{1,0:T(8,128)}, u32[]{:S(2)}, u32[]{:S(2)}) collective-permute-start(f32[896,896]{1,0:T(8,128)} %param.9), channel_id=1, source_target_pairs={{0,16},{1,17},{2,18},{3,19},{4,20},{5,21},{6,22},{7,23},{8,24},{9,... | collective-permute-start | bytes 9633800 | tf_op jit(solution)/shard_map/ppermute | solution.py:10
  324.9 0.0 copy-done.8
  324.9 0.5 fusion.26
  330.7 0.0 copy-done.6
  330.7 0.1 copy.23
  330.8 0.0 copy-done.7
  330.8 0.1 copy.27
  330.9 0.1 broadcast_in_dim.14
  331.0 0.1 broadcast_in_dim.12
  331.2 5.8 %copy.22 = bf16[1,2,896,896]{2,3,1,0:T(8,128)(2,1)} copy(bf16[1,2,896,896]{3,2,1,0:T(8,128)(2,1)} %param.13) | data formatting | bytes 6422528 | tf_op args[4]
  337.0 2.3 convert_multiply_fusion.1
  339.3 0.0 collective-permute-done.2
  339.3 0.0 collective-permute-done.1
  339.3 0.0 collective-permute-done
  339.3 13.2 %fusion.2 = f32[896,896]{1,0:T(8,128)} fusion(f32[2,896,896]{1,2,0:T(8,128)S(1)} %convert_multiply_fusion.1, f32[896,896]{1,0:T(8,128)} %collective-permute-done, f32[896,896]{1,0:T(8,128)} %collective-permute-done.1, f32[896,896]{1,0:T(8,128)S(1)} %collective-permute-done.2, pred[]{:T(512)S(6)} %eq.53, pred[]{:T(512)S(6)} %eq.52, pred[]{:T(512)S(6)} %eq.51), kind=kOutput, calls=%fused_computation.7 | convolution fusion | flops 8634286080 | bytes 16056323 | tf_op jit(solution)/shard_map/dot_general | solution.py:55
  352.5 14.7 %fusion.3 = f32[896,896]{1,0:T(8,128)} fusion(f32[2,896,896]{1,2,0:T(8,128)S(1)} %convert_multiply_fusion.1, f32[896,896]{1,0:T(8,128)} %collective-permute-done, f32[896,896]{1,0:T(8,128)} %collective-permute-done.1, f32[896,896]{1,0:T(8,128)S(1)} %collective-permute-done.2, pred[]{:T(512)S(6)} %eq.50, pred[]{:T(512)S(6)} %eq.49, pred[]{:T(512)S(6)} %eq.48), kind=kOutput, calls=%fused_computation.9 | convolution fusion | flops 8634286080 | bytes 16056323 | tf_op jit(solution)/shard_map/dot_general | solution.py:54
  367.2 8.6 %copy.26 = bf16[1,2,896,896]{2,3,1,0:T(8,128)(2,1)S(1)} copy(bf16[1,2,896,896]{3,1,0,2:T(2,128)(2,1)} %all-gather.2.cloned.1.call-done) | data formatting | bytes 6422528 | tf_op jit(solution)/shard_map/all_gather | solution.py:35
  375.8 0.0 copy-start.2
  375.8 0.4 convert_multiply_fusion
  376.3 0.0 copy-start
  376.3 0.0 copy-start.4
  376.3 88.1 %collective-permute-done.7 = f32[896,896]{1,0:T(8,128)} collective-permute-done((f32[896,896]{1,0:T(8,128)}, f32[896,896]{1,0:T(8,128)}, u32[]{:S(2)}, u32[]{:S(2)}) %collective-permute-start.7) | collective-permute-done | bytes 3211296 | tf_op jit(solution)/shard_map/ppermute | solution.py:10
  464.5 12.2 %fusion = f32[896,896]{1,0:T(8,128)S(1)} fusion(f32[2,896,896]{1,2,0:T(8,128)S(1)} %convert_multiply_fusion, f32[896,896]{1,0:T(8,128)} %collective-permute-done.7, f32[896,896]{1,0:T(8,128)S(1)} %copy-done.2, pred[]{:T(512)S(6)} %eq.63), kind=kOutput, calls=%fused_computation.3 | convolution fusion | flops 8632680448 | bytes 12845057 | tf_op jit(solution)/shard_map/dot_general | solution.py:39
  476.7 15.4 %add_divide_fusion = f32[896,896]{1,0:T(8,128)} fusion(f32[896,896]{1,0:T(8,128)S(1)} %copy-done.4, f32[896,896]{1,0:T(8,128)} %param.9, f32[896,896]{1,0:T(8,128)S(1)} %fusion, f32[896,896]{1,0:T(8,128)S(1)} %copy-done.1, f32[896,896]{1,0:T(8,128)S(1)} %copy-done, f32[]{:T(128)} %bitcast.37, f32[2,896,896]{1,2,0:T(8,128)S(1)} %convert_multiply_fusion, ...), kind=kOutput, calls=%fused_computation.10 | convolution fusion | flops 8640708608 | bytes 28901380 | tf_op jit(solution)/shard_map/dot_general | solution.py:38
  (14 shorter events, 0.1 us)
Async XLA Ops:
  6.5 360.7 %all-gather.2.cloned.1.call-start = ((), (), s32[]{:S(2)}) async-start(), calls=%async_computation | async-start | bytes 3612672 | tf_op jit(solution)/shard_map/all_gather | solution.py:35
  6.5 6.1 %collective-permute-start.3 = (f32[896,896]{1,0:T(8,128)}, f32[896,896]{1,0:T(8,128)}, u32[]{:S(2)}, u32[]{:S(2)}) collective-permute-start(f32[896,896]{1,0:T(8,128)} %param.9), channel_id=1, source_target_pairs={{0,1},{1,0},{2,3},{3,2},{4,5},{5,4},{6,7},{7,6},{8,9},{9,8},{10,11... | collective-permute-start | bytes 9633800 | tf_op jit(solution)/shard_map/ppermute | solution.py:10
  16.6 71.9 %collective-permute-start.4 = (f32[896,896]{1,0:T(8,128)}, f32[896,896]{1,0:T(8,128)}, u32[]{:S(2)}, u32[]{:S(2)}) collective-permute-start(f32[896,896]{1,0:T(8,128)} %param.9), channel_id=1, source_target_pairs={{0,2},{1,3},{2,0},{3,1},{4,6},{5,7},{6,4},{7,5},{8,10},{9,11},{10,... | collective-permute-start | bytes 9633800 | tf_op jit(solution)/shard_map/ppermute | solution.py:10
  94.6 71.1 %collective-permute-start.5 = (f32[896,896]{1,0:T(8,128)}, f32[896,896]{1,0:T(8,128)S(1)}, u32[]{:S(2)}, u32[]{:S(2)}) collective-permute-start(f32[896,896]{1,0:T(8,128)} %param.9), channel_id=1, source_target_pairs={{0,4},{1,5},{2,6},{3,7},{4,0},{5,1},{6,2},{7,3},{8,12},{9,13},{10,... | collective-permute-start | bytes 9633800 | tf_op jit(solution)/shard_map/ppermute | solution.py:10
  97.8 76.4 %copy-start.5 = (bf16[1,2,112,896]{3,2,1,0:T(8,128)(2,1)S(1)}, bf16[1,2,112,896]{3,2,1,0:T(8,128)(2,1)}, u32[]{:S(2)}) copy-start(bf16[1,2,112,896]{3,2,1,0:T(8,128)(2,1)} %param.16) | copy-start | bytes 1204228
  170.9 140.9 %collective-permute-start.6 = (f32[896,896]{1,0:T(8,128)}, f32[896,896]{1,0:T(8,128)}, u32[]{:S(2)}, u32[]{:S(2)}) collective-permute-start(f32[896,896]{1,0:T(8,128)} %param.9), channel_id=1, source_target_pairs={{0,8},{1,9},{2,10},{3,11},{4,12},{5,13},{6,14},{7,15},{8,0},{9,1},... | collective-permute-start | bytes 9633800 | tf_op jit(solution)/shard_map/ppermute | solution.py:10
  175.3 164.0 %collective-permute-start.2 = (f32[896,896]{1,0:T(8,128)}, f32[896,896]{1,0:T(8,128)S(1)}, u32[]{:S(2)}, u32[]{:S(2)}) collective-permute-start(f32[896,896]{1,0:T(8,128)} %param.9), channel_id=1, source_target_pairs={{0,32},{32,0},{64,96},{96,64},{128,160},{160,128},{192,224},{224,1... | collective-permute-start | bytes 9633800 | tf_op jit(solution)/shard_map/ppermute | solution.py:10
  177.0 162.3 %collective-permute-start.1 = (f32[896,896]{1,0:T(8,128)}, f32[896,896]{1,0:T(8,128)}, u32[]{:S(2)}, u32[]{:S(2)}) collective-permute-start(f32[896,896]{1,0:T(8,128)} %param.9), channel_id=1, source_target_pairs={{0,64},{32,96},{64,0},{96,32},{128,192},{160,224},{192,128},{224,1... | collective-permute-start | bytes 9633800 | tf_op jit(solution)/shard_map/ppermute | solution.py:10
  179.9 159.4 %collective-permute-start = (f32[896,896]{1,0:T(8,128)}, f32[896,896]{1,0:T(8,128)}, u32[]{:S(2)}, u32[]{:S(2)}) collective-permute-start(f32[896,896]{1,0:T(8,128)} %param.9), channel_id=1, source_target_pairs={{0,128},{32,160},{64,192},{96,224},{128,0},{160,32},{192,64},{224,... | collective-permute-start | bytes 9633800 | tf_op jit(solution)/shard_map/ppermute | solution.py:10
  181.6 143.2 %copy-start.8 = (s32[1,2]{1,0:T(1,128)S(1)}, s32[1,2]{1,0:T(1,128)}, u32[]{:S(2)}) copy-start(s32[1,2]{1,0:T(1,128)} %param.12) | copy-start | bytes 28
  181.7 149.0 %copy-start.6 = (s32[1,2,7,7]{3,1,2,0:T(2,128)S(1)}, s32[1,2,7,7]{3,1,2,0:T(2,128)}, u32[]{:S(2)}) copy-start(s32[1,2,7,7]{3,1,2,0:T(2,128)} %param.14) | copy-start | bytes 1180
  181.7 149.1 %copy-start.7 = (s32[1,2,7,7]{3,1,2,0:T(2,128)S(1)}, s32[1,2,7,7]{3,1,2,0:T(2,128)}, u32[]{:S(2)}) copy-start(s32[1,2,7,7]{3,1,2,0:T(2,128)} %param.17) | copy-start | bytes 1180
  318.9 145.5 %collective-permute-start.7 = (f32[896,896]{1,0:T(8,128)}, f32[896,896]{1,0:T(8,128)}, u32[]{:S(2)}, u32[]{:S(2)}) collective-permute-start(f32[896,896]{1,0:T(8,128)} %param.9), channel_id=1, source_target_pairs={{0,16},{1,17},{2,18},{3,19},{4,20},{5,21},{6,22},{7,23},{8,24},{9,... | collective-permute-start | bytes 9633800 | tf_op jit(solution)/shard_map/ppermute | solution.py:10
  375.8 88.6 %copy-start.2 = (f32[896,896]{1,0:T(8,128)S(1)}, f32[896,896]{1,0:T(8,128)}, u32[]{:S(2)}) copy-start(f32[896,896]{1,0:T(8,128)} %get-tuple-element.13) | copy-start | bytes 9633796
  376.3 100.4 %copy-start = (f32[896,896]{1,0:T(8,128)S(1)}, f32[896,896]{1,0:T(8,128)}, u32[]{:S(2)}) copy-start(f32[896,896]{1,0:T(8,128)} %fusion.2) | copy-start | bytes 9633796
  376.3 100.4 %copy-start.1 = (f32[896,896]{1,0:T(8,128)S(1)}, f32[896,896]{1,0:T(8,128)}, u32[]{:S(2)}) copy-start(f32[896,896]{1,0:T(8,128)} %fusion.3) | copy-start | bytes 9633796
  376.3 100.4 %copy-start.3 = (f32[896,896]{1,0:T(8,128)S(1)}, f32[896,896]{1,0:T(8,128)}, u32[]{:S(2)}) copy-start(f32[896,896]{1,0:T(8,128)} %get-tuple-element.14) | copy-start | bytes 9633796
  376.3 100.4 %copy-start.4 = (f32[896,896]{1,0:T(8,128)S(1)}, f32[896,896]{1,0:T(8,128)}, u32[]{:S(2)}) copy-start(f32[896,896]{1,0:T(8,128)} %param.10) | copy-start | bytes 9633796
Sparse Core Ops, SparseCore 0:
  175.4 93.5 all-gather.1
where the time goes:
time: 508 us; the launch traced here: 499 us
  waiting for transfers between devices  359 us (71%)
  matrix products  55.5 us (11%)
  other arithmetic  25.2 us (5%)
  between operations  24.1 us (5%)
  local copies, waits for them, and re-layouts  17.8 us (4%)
  starting transfers between devices  17.4 us (3%)
    ppermute x8, waiting for transfers between devices, from_partner(): lax.ppermute(value, axis, [(i, i ^ 1 << apart) for i in range(lax.axis_si...  359 us
    select_n x4, other arithmetic, beta_part(): second_tile = jnp.where(beta_partner[0, 1] == source, arrived, second_tile)  22.4 us
    ppermute x8, starting transfers between devices, from_partner(): lax.ppermute(value, axis, [(i, i ^ 1 << apart) for i in range(lax.axis_si...  17.4 us
    dot_general x1, matrix products, beta_part(): summed = jnp.dot(first_tile, weights[0], precision=highest)  15.4 us
    dot_general x1, matrix products, alpha_part(): summed = jnp.dot(weights[0].T, first_rows, precision=highest)  14.7 us
    dot_general x1, matrix products, alpha_part(): return summed + jnp.dot(weights[1].T, second_rows, precision=highest)  13.2 us
    dot_general x1, matrix products, beta_part(): return summed + jnp.dot(second_tile, weights[1], precision=highest)  12.2 us
  transfers between devices with their start and end apart: 9, of which 5 were waited for; matrix products, arithmetic and copies ran while one was open for 11% of the time, Pallas kernels for 0%

commit v1 on v0

v1 whole, which is shorter than its diff:
```python
import jax
import jax.numpy as jnp
from jax import lax
from jax.experimental import pallas as pl
from jax.experimental.pallas import tpu as pltpu
from jax.sharding import PartitionSpec as P

MESH = pl.DeviceIdType.MESH
TILE = 896
BLOCK = 128
NBLK = TILE // BLOCK
HEAD = 16
CHUNKS = 7
ROWS = TILE // CHUNKS
PIECE = 112
LEVELS = 32767.0
F32 = jnp.float32
BF16 = jnp.bfloat16
K0, X1, X2, Y1, Y2, Z2, Z3, Z4 = range(8)
ZR = 8


def chunk_rows(c):
    return pl.ds(0, HEAD + ROWS) if c == 0 else pl.ds(HEAD + ROWS * c, ROWS)


def data_rows(c):
    return pl.ds(HEAD + ROWS * c, ROWS)


def flipped(index, bit):
    return index + (1 - 2 * ((index // bit) % 2)) * bit


def split(value):
    high = value.astype(BF16)
    return high, (value - high.astype(F32)).astype(BF16)


def pick(choices, rows):
    value = choices[0][1][rows, :]
    for chosen, ref in choices[1:]:
        value = lax.select(chosen, ref[rows, :], value)
    return value.astype(F32)


def decode(choices, rows):
    scale = jnp.exp2(pick(choices, pl.ds(0, HEAD)))[0:1, :]
    root = pick(choices, rows) * (1.0 / LEVELS)
    return (root * jnp.abs(root)) * (root * root) * scale


def kernel(
    ci_hbm, ac_hbm, bc_hbm, am, bm, ap, bp, out_hbm,
    cv, own, k0, x1, x2, y1, y2, z2, z3, z4, weights, piece, ha, hat, bl, xl, part, acc,
    load_sem, send_sem, recv_sem, wsend_sem, wrecv_sem, store_sem,
):
    tiles = [k0, x1, x2, y1, y2, z2, z3, z4]
    a = lax.axis_index("alpha")
    b = lax.axis_index("beta")
    y, xh = a % 4, a // 4
    core, xl_, z = b % 2, (b // 2) % 2, b // 4
    x = xh * 2 + xl_

    def at(dx=0, dy=0, dz=0, dc=0):
        nx, ny, nz = (x + dx + 4) % 4, (y + dy + 4) % 4, (z + dz + 8) % 8
        nc = (core + dc) % 2
        return ((nx // 2) * 4 + ny, nz * 4 + (nx % 2) * 2 + nc)

    tx = 1 - 2 * (x % 2)
    ty = 1 - 2 * (y % 2)
    tz = 1 - 2 * (z % 2)
    t = z % 4
    sz = 1 - 2 * (t // 2)
    inner = (t == 1) | (t == 2)

    load_c = pltpu.make_async_copy(ci_hbm, cv, load_sem.at[0])
    load_p = pltpu.make_async_copy(bc_hbm.at[0], piece, load_sem.at[1])
    load_a = pltpu.make_async_copy(ac_hbm.at[0], ha, load_sem.at[2])
    load_c.start()
    load_p.start()
    load_a.start()

    barrier = pltpu.get_barrier_semaphore()
    greet = [at(dc=1), at(dx=1), at(dx=-1), at(dx=2), at(dy=1), at(dy=-1), at(dz=1), at(dz=-1), at(dz=2), at(dz=-2)]
    for other in greet:
        pl.semaphore_signal(barrier, inc=1, device_id=other, device_id_type=MESH)

    def move(src, dst, lane, c, target):
        rows = chunk_rows(c)
        return pltpu.make_async_remote_copy(
            src_ref=src.at[rows, :],
            dst_ref=tiles[dst].at[rows, :],
            send_sem=send_sem.at[lane, c],
            recv_sem=recv_sem.at[dst, c],
            device_id=target,
            device_id_type=MESH,
        )

    def own_to_core(c):
        return move(own, K0, K0, c, at(dc=1))

    def own_to_x(c):
        return move(own, X1, X1, c, at(dx=tx))

    def pass_x(c):
        return move(x1, X2, X2, c, at(dx=-tx))

    def own_to_y(c):
        return move(own, Y1, Y1, c, at(dy=ty))

    def pass_y(c):
        return move(y1, Y2, Y2, c, at(dy=-ty))

    def own_to_z(c):
        return move(own, Z2, Z2, c, at(dz=tz))

    def own_to_z_far(c):
        return move(own, Z3, Z3, c, at(dz=2 * sz))

    def pass_z(c):
        return move(z2, Z3, ZR, c, at(dz=sz))

    def pass_z_far(c):
        return move(z3, Z4, Z4, c, at(dz=-2 * sz))

    def arrived(dst, c):
        rows = chunk_rows(c)
        pltpu.make_async_remote_copy(
            src_ref=tiles[dst].at[rows, :],
            dst_ref=tiles[dst].at[rows, :],
            send_sem=send_sem.at[dst, c],
            recv_sem=recv_sem.at[dst, c],
            device_id=at(dc=1),
            device_id_type=MESH,
        ).wait_recv()

    def wmove(ah, dy_src, lane, target):
        index = ((xh + ah) % 2) * 4 + (y + dy_src + 4) % 4
        rows = pl.ds(pl.multiple_of(index * PIECE, 16), PIECE)
        return pltpu.make_async_remote_copy(
            src_ref=weights.at[:, rows, :],
            dst_ref=weights.at[:, rows, :],
            send_sem=wsend_sem.at[lane],
            recv_sem=wrecv_sem.at[lane],
            device_id=target,
            device_id_type=MESH,
        )

    wsend = [
        wmove(0, 0, 0, at(dx=2)),
        wmove(0, 0, 1, at(dy=1)),
        wmove(0, 0, 2, at(dy=-1)),
        wmove(1, 0, 3, at(dy=1)),
        wmove(1, 0, 4, at(dy=-1)),
        wmove(0, -1, 5, at(dy=1)),
        wmove(1, 1, 6, at(dy=-1)),
    ]
    wrecv = [
        wmove(1, 0, 0, at(dx=2)),
        wmove(0, -1, 1, at(dy=1)),
        wmove(0, 1, 2, at(dy=1)),
        wmove(1, -1, 3, at(dy=1)),
        wmove(1, 1, 4, at(dy=1)),
        wmove(0, -2, 5, at(dy=1)),
        wmove(1, 2, 6, at(dy=1)),
    ]

    load_c.wait()

    def biggest(c, value):
        return jnp.maximum(value, jnp.max(jnp.abs(cv[pl.ds(pl.multiple_of(c * ROWS, ROWS), ROWS), :]), axis=0, keepdims=True))

    column = lax.fori_loop(0, CHUNKS, biggest, jnp.full((1, TILE), 1e-36, F32))
    top = jnp.max(column, axis=1, keepdims=True)
    exponent = jnp.maximum(jnp.floor(jnp.log2(top)) + 1.0, -120.0)
    exponent = jnp.broadcast_to(exponent, (HEAD, TILE))
    own[pl.ds(0, HEAD), :] = exponent.astype(jnp.int16)
    shrink = jnp.exp2(-exponent[0:1, :])

    def encode(c):
        value = cv[pl.ds(c * ROWS, ROWS), :]
        root = jnp.sqrt(jnp.sqrt(jnp.abs(value) * shrink)) * LEVELS
        root = jnp.minimum(jnp.round(root), LEVELS)
        own[data_rows(c), :] = jnp.where(value < 0, -root, root).astype(jnp.int16)

    def send_z(c):
        own_to_z(c).start()

        @pl.when(inner)
        def _():
            own_to_z_far(c).start()

    encode(0)
    pl.semaphore_wait(barrier, len(greet))
    send_z(0)
    encode(1)
    send_z(1)

    load_p.wait()
    for s in range(2):
        for k in range(PIECE // 16):
            row = a * PIECE + 16 * k
            u = row // BLOCK
            rows = pl.ds(pl.multiple_of(row, 16), 16)
            for v in range(NBLK):
                columns = pl.ds(v * BLOCK, BLOCK)
                block = piece[s, pl.ds(16 * k, 16), columns].astype(F32)
                weights[s, rows, columns] = (block * bm[0, s, u, v].astype(F32)).astype(BF16)
    for lane in (0, 1, 2):
        wsend[lane].start()
    for c in range(CHUNKS):
        if c >= 2:
            encode(c)
        own_to_x(c).start()
        own_to_y(c).start()
        own_to_core(c).start()

    load_a.wait()

    def mask_alpha(i, _):
        s, u = i // NBLK, i % NBLK
        rows = pl.ds(pl.multiple_of(u * BLOCK, BLOCK), BLOCK)
        to = pl.ds(pl.multiple_of(s * TILE + u * BLOCK, BLOCK), BLOCK)
        for v in range(NBLK):
            block = ha[s, rows, pl.ds(v * BLOCK, BLOCK)].astype(F32) * am[0, s, u, v].astype(F32)
            hat[pl.ds(v * BLOCK, BLOCK), to] = block.T.astype(BF16)
        return 0

    lax.fori_loop(0, 2 * NBLK, mask_alpha, 0)

    alpha_from = [[(ap[0, s] == flipped(a, bit), ref) for bit, ref in ((1, y1), (2, y2), (4, x2))] for s in range(2)]
    beta_from = [[(bp[0, s] == flipped(b, bit), ref) for bit, ref in ((1, k0), (2, x1), (4, z2), (8, z3), (16, z4))] for s in range(2)]

    def alpha_operand():
        def body(c, _):
            rows = pl.ds(pl.multiple_of(HEAD + c * ROWS, 16), ROWS)
            for s in range(2):
                high, low = split(decode(alpha_from[s], rows))
                to = pl.ds(pl.multiple_of(s * TILE + c * ROWS, ROWS), ROWS)
                for n in range(NBLK):
                    bl[n, to, pl.ds(0, BLOCK)] = high[:, n * BLOCK : (n + 1) * BLOCK]
                    bl[n, to, pl.ds(BLOCK, BLOCK)] = low[:, n * BLOCK : (n + 1) * BLOCK]
            return 0

        lax.fori_loop(0, CHUNKS, body, 0)

    def alpha_product(first, last):
        def body(i, _):
            n, m = i // 2, i % 2
            rows = pl.ds(pl.multiple_of(m * 448, 64), 448)
            both = jnp.dot(hat[rows, :], bl[n], preferred_element_type=F32)
            acc[rows, pl.ds(pl.multiple_of(n * BLOCK, BLOCK), BLOCK)] = both[:, :BLOCK] + both[:, BLOCK:]
            return 0

        lax.fori_loop(2 * first, 2 * last, body, 0)

    def beta_product(c):
        for s in range(2):
            high, low = split(decode(beta_from[s], data_rows(c)))
            xl[s, pl.ds(0, ROWS), :] = high
            xl[s, pl.ds(ROWS, ROWS), :] = low

        part[...] = jnp.zeros_like(part)
        for s in range(2):
            for k in (pl.ds(0, 512), pl.ds(512, TILE - 512)):
                part[...] += jnp.dot(xl[s, :, k], weights[s, k, :], preferred_element_type=F32)
        rows = pl.ds(c * ROWS, ROWS)
        acc[rows, :] = acc[rows, :] + (part[pl.ds(0, ROWS), :] + part[pl.ds(ROWS, ROWS), :])

    def store(c):
        rows = pl.ds(c * ROWS, ROWS)
        return pltpu.make_async_copy(acc.at[rows, :], out_hbm.at[rows, :], store_sem.at[c])

    for step in range(CHUNKS + 4):
        if 2 <= step + 1 < CHUNKS:
            send_z(step + 1)
        c = step - 1
        if 0 <= c < CHUNKS:

            @pl.when(inner)
            def _():
                arrived(Z2, c)
                pass_z(c).start()

        c = step - 2
        if 0 <= c < CHUNKS:
            arrived(Z3, c)
            pass_z_far(c).start()
        for c in (2 * step - 1, 2 * step):
            if 0 <= c < CHUNKS:
                arrived(X1, c)
                pass_x(c).start()
                arrived(Y1, c)
                pass_y(c).start()
        if step == 0:
            wrecv[0].wait_recv()
            wsend[3].start()
            wsend[4].start()
            wrecv[1].wait_recv()
            wsend[5].start()
        if step == 1:
            wrecv[4].wait_recv()
            wsend[6].start()
        if step == 4:
            for c in range(CHUNKS):
                arrived(X2, c)
                arrived(Y2, c)
            alpha_operand()
            alpha_product(0, 3)
            for lane in (2, 3, 5, 6):
                wrecv[lane].wait_recv()
        if step == 5:
            alpha_product(3, NBLK)
        for c in range(CHUNKS):
            if step == max(c + 4, 5):
                arrived(K0, c)

                @pl.when(jnp.logical_not(inner))
                def _():
                    arrived(Z2, c)

                arrived(Z4, c)
                beta_product(c)
                store(c).start()

    for c in range(CHUNKS):
        store(c).wait()
        for copy in (own_to_core(c), own_to_x(c), pass_x(c), own_to_y(c), pass_y(c), own_to_z(c), pass_z_far(c)):
            copy.wait_send()

        @pl.when(inner)
        def _():
            own_to_z_far(c).wait_send()
            pass_z(c).wait_send()

    for copy in wsend:
        copy.wait_send()


def local(ci_vector, diagonal, energy, alpha_partner, alpha_coupling, alpha_mask, beta_partner, beta_coupling, beta_mask):
    anywhere = pl.BlockSpec(memory_space=pl.ANY)
    scalars = pl.BlockSpec(memory_space=pltpu.SMEM)
    code = pltpu.VMEM((HEAD + TILE, TILE), jnp.int16)
    sigma = pl.pallas_call(
        kernel,
        out_shape=jax.ShapeDtypeStruct((TILE, TILE), F32),
        in_specs=[anywhere] * 3 + [scalars] * 4,
        out_specs=anywhere,
        scratch_shapes=[pltpu.VMEM((TILE, TILE), F32)]
        + [code] * 9
        + [
            pltpu.VMEM((2, TILE, TILE), BF16),
            pltpu.VMEM((2, PIECE, TILE), BF16),
            pltpu.VMEM((2, TILE, TILE), BF16),
            pltpu.VMEM((TILE, 2 * TILE), BF16),
            pltpu.VMEM((NBLK, 2 * TILE, 2 * BLOCK), BF16),
            pltpu.VMEM((2, 2 * ROWS, TILE), BF16),
            pltpu.VMEM((2 * ROWS, TILE), F32),
            pltpu.VMEM((TILE, TILE), F32),
            pltpu.SemaphoreType.DMA((3,)),
            pltpu.SemaphoreType.DMA((9, CHUNKS)),
            pltpu.SemaphoreType.DMA((8, CHUNKS)),
            pltpu.SemaphoreType.DMA((7,)),
            pltpu.SemaphoreType.DMA((7,)),
            pltpu.SemaphoreType.DMA((CHUNKS,)),
        ],
        compiler_params=pltpu.CompilerParams(collective_id=0, has_side_effects=True, vmem_limit_bytes=60 * 1024 * 1024),
    )(ci_vector, alpha_coupling, beta_coupling, alpha_mask, beta_mask, alpha_partner, beta_partner)
    gap = diagonal - energy[0]
    return (sigma - energy[0] * ci_vector) * gap / (gap * gap + 0.0625)


def solution(mesh):
    return jax.shard_map(
        local,
        mesh=mesh,
        in_specs=(
            P("alpha", "beta"),
            P("alpha", "beta"),
            P(),
            P("alpha", None),
            P("alpha", None, None, None),
            P("alpha", None, None, None),
            P("beta", None),
            P("beta", None, "alpha", None),
            P("beta", None, None, None),
        ),
        out_specs=P("alpha", "beta"),
        check_vma=False,
    )
```

time: 508 us -> 159 us (0.31); the launches traced: 499 us -> 156 us
  waiting for transfers between devices: 359 us -> 0 us
  Pallas kernels: 0 us -> 147 us
  matrix products: 55.5 us -> 0 us
  between operations: 24.1 us -> 0.67 us
  other arithmetic: 25.2 us -> 5.41 us
  starting transfers between devices: 17.4 us -> 0 us
  local copies, waits for them, and re-layouts: 17.8 us -> 2.57 us
    ppermute x8 -> x0, waiting for transfers between devices: 359 us -> none  [from_partner(): lax.ppermute(value, axis, [(i, i ^ 1 << apart) for i in range(lax.axis_si...]
    pallas_call x0 -> x1, Pallas kernels: none -> 147 us  [local(): pl.pallas_call(kernel, out_shape=jax.ShapeDtypeStruct((TILE, TILE), F32),...]
    dot_general x4 -> x0, matrix products: 55.5 us -> none  [the longest x1 15.4 us: beta_part(): summed = jnp.dot(first_tile, weights[0], precision=highest)]
    select_n x4 -> x0, other arithmetic: 22.4 us -> none  [beta_part(): second_tile = jnp.where(beta_partner[0, 1] == source, arrived, second_tile)]
    ppermute x8 -> x0, starting transfers between devices: 17.4 us -> none  [from_partner(): lax.ppermute(value, axis, [(i, i ^ 1 << apart) for i in range(lax.axis_si...]
    all_gather x1 -> x0, local copies, waits for them, and re-layouts: 8.58 us -> none  [beta_part(): lax.all_gather(beta_coupling, 'alpha', axis=2, tiled=True)[0]]
    div x0 -> x1, other arithmetic: none -> 5.41 us  [local(): return (sigma - energy[0] * ci_vector) * gap / (gap * gap + 0.0625)]
  transfers between devices with their start and end apart: 9 -> 0, of which waited for: 5 -> 0; matrix products, arithmetic and copies ran while one was open for 11% -> 0% of each run, Pallas kernels for 0% -> 0%
where the time goes in v1:
time: 159 us; the launch traced here: 156 us
  Pallas kernels  147 us (92%)
  other arithmetic  5.41 us (3%)
  local copies, waits for them, and re-layouts  2.57 us (2%)
    pallas_call x1, Pallas kernels, local(): pl.pallas_call(kernel, out_shape=jax.ShapeDtypeStruct((TILE, TILE), F32),...  147 us
    div x1, other arithmetic, local(): return (sigma - energy[0] * ci_vector) * gap / (gap * gap + 0.0625)  5.41 us

profile of v1, /device:TPU:4, one launch (start us, length us, event | category | flops | bytes accessed | tf_op | source)
XLA Modules:
  0.0 156.1 jit_solution(10560010230206794204)
XLA Ops:
  0.0 1.3 copy.10.am
  1.3 1.3 copy.11.bm
  2.6 0.0 copy-start
  2.6 147.4 %shard_map.91 = f32[896,896]{1,0:T(8,128)} custom-call(f32[896,896]{1,0:T(8,128)} %ci_hbm.1, bf16[1,2,896,896]{3,2,1,0:T(8,128)(2,1)} %ac_hbm.1, bf16[1,2,112,896]{3,2,1,0:T(8,128)(2,1)} %bc_hbm.1, s32[1,2,7,7]{3,2,1,0:T(8,128)} %copy.10.am, s32[1,2,7,7]{3,2,1,0:T(8,128)} %copy.11.bm, s32[1,2]{1,0:T(1,128)} %ap.1, s32[1,2]{1,0:T(1,128)} %bp.1), custom_call_target="tpu_custom_call" | custom-call | tf_op jit(solution)/shard_map/pallas_call | solution.py:345
  150.6 0.0 copy-done
  150.7 5.4 %add_divide_fusion = f32[896,896]{1,0:T(8,128)} fusion(f32[896,896]{1,0:T(8,128)} %param.10, f32[896,896]{1,0:T(8,128)} %shard_map.91, f32[896,896]{1,0:T(8,128)S(1)} %copy-done, f32[]{:T(128)} %bitcast.1), kind=kLoop, calls=%fused_computation | loop fusion | flops 5619712 | bytes 12845060 | tf_op jit(solution)/shard_map/div | solution.py:371
Async XLA Ops:
  2.6 148.1 %copy-start = (f32[896,896]{1,0:T(8,128)S(1)}, f32[896,896]{1,0:T(8,128)}, u32[]{:S(2)}) copy-start(f32[896,896]{1,0:T(8,128)} %ci_hbm.1) | copy-start | bytes 9633796

commit v2 on v1

--- a/solution.py
+++ b/solution.py
@@ -10,8 +10,10 @@
 BLOCK = 128
 NBLK = TILE // BLOCK
 HEAD = 16
-CHUNKS = 7
+CHUNKS = 14
 ROWS = TILE // CHUNKS
+PARTS = 7
+PROWS = TILE // PARTS
 PIECE = 112
 LEVELS = 32767.0
 F32 = jnp.float32
@@ -51,8 +53,8 @@
 
 
 def kernel(
-    ci_hbm, ac_hbm, bc_hbm, am, bm, ap, bp, out_hbm,
-    cv, own, k0, x1, x2, y1, y2, z2, z3, z4, weights, piece, ha, hat, bl, xl, part, acc,
+    ci_hbm, diag_hbm, ac_hbm, bc_hbm, am, bm, ap, bp, energy, out_hbm,
+    cv, dv, own, k0, x1, x2, y1, y2, z2, z3, z4, weights, piece, ha, hat, bl, xl, part, acc,
     load_sem, send_sem, recv_sem, wsend_sem, wrecv_sem, store_sem,
 ):
     tiles = [k0, x1, x2, y1, y2, z2, z3, z4]
@@ -77,9 +79,11 @@
     load_c = pltpu.make_async_copy(ci_hbm, cv, load_sem.at[0])
     load_p = pltpu.make_async_copy(bc_hbm.at[0], piece, load_sem.at[1])
     load_a = pltpu.make_async_copy(ac_hbm.at[0], ha, load_sem.at[2])
+    load_d = pltpu.make_async_copy(diag_hbm, dv, load_sem.at[3])
     load_c.start()
     load_p.start()
     load_a.start()
+    load_d.start()
 
     barrier = pltpu.get_barrier_semaphore()
     greet = [at(dc=1), at(dx=1), at(dx=-1), at(dx=2), at(dy=1), at(dy=-1), at(dz=1), at(dz=-1), at(dz=2), at(dz=-2)]
@@ -169,9 +173,9 @@
     load_c.wait()
 
     def biggest(c, value):
-        return jnp.maximum(value, jnp.max(jnp.abs(cv[pl.ds(pl.multiple_of(c * ROWS, ROWS), ROWS), :]), axis=0, keepdims=True))
-
-    column = lax.fori_loop(0, CHUNKS, biggest, jnp.full((1, TILE), 1e-36, F32))
+        return jnp.maximum(value, jnp.max(jnp.abs(cv[pl.ds(pl.multiple_of(c * PROWS, PROWS), PROWS), :]), axis=0, keepdims=True))
+
+    column = lax.fori_loop(0, PARTS, biggest, jnp.full((1, TILE), 1e-36, F32))
     top = jnp.max(column, axis=1, keepdims=True)
     exponent = jnp.maximum(jnp.floor(jnp.log2(top)) + 1.0, -120.0)
     exponent = jnp.broadcast_to(exponent, (HEAD, TILE))
@@ -185,17 +189,20 @@
         own[data_rows(c), :] = jnp.where(value < 0, -root, root).astype(jnp.int16)
 
     def send_z(c):
-        own_to_z(c).start()
-
         @pl.when(inner)
         def _():
             own_to_z_far(c).start()
 
+        @pl.when(jnp.logical_not(inner))
+        def _():
+            own_to_z(c).start()
+
     encode(0)
     pl.semaphore_wait(barrier, len(greet))
     send_z(0)
-    encode(1)
-    send_z(1)
+    for c in range(1, CHUNKS):
+        encode(c)
+        send_z(c)
 
     load_p.wait()
     for s in range(2):
@@ -210,40 +217,33 @@
     for lane in (0, 1, 2):
         wsend[lane].start()
     for c in range(CHUNKS):
-        if c >= 2:
-            encode(c)
         own_to_x(c).start()
         own_to_y(c).start()
         own_to_core(c).start()
 
     load_a.wait()
 
-    def mask_alpha(i, _):
+    def mask_alpha(i):
         s, u = i // NBLK, i % NBLK
-        rows = pl.ds(pl.multiple_of(u * BLOCK, BLOCK), BLOCK)
-        to = pl.ds(pl.multiple_of(s * TILE + u * BLOCK, BLOCK), BLOCK)
         for v in range(NBLK):
-            block = ha[s, rows, pl.ds(v * BLOCK, BLOCK)].astype(F32) * am[0, s, u, v].astype(F32)
-            hat[pl.ds(v * BLOCK, BLOCK), to] = block.T.astype(BF16)
-        return 0
-
-    lax.fori_loop(0, 2 * NBLK, mask_alpha, 0)
+            block = ha[s, pl.ds(u * BLOCK, BLOCK), pl.ds(v * BLOCK, BLOCK)].astype(F32) * am[0, s, u, v].astype(F32)
+            hat[pl.ds(v * BLOCK, BLOCK), pl.ds(s * TILE + u * BLOCK, BLOCK)] = block.T.astype(BF16)
 
     alpha_from = [[(ap[0, s] == flipped(a, bit), ref) for bit, ref in ((1, y1), (2, y2), (4, x2))] for s in range(2)]
     beta_from = [[(bp[0, s] == flipped(b, bit), ref) for bit, ref in ((1, k0), (2, x1), (4, z2), (8, z3), (16, z4))] for s in range(2)]
 
     def alpha_operand():
         def body(c, _):
-            rows = pl.ds(pl.multiple_of(HEAD + c * ROWS, 16), ROWS)
+            rows = pl.ds(pl.multiple_of(HEAD + c * PROWS, 16), PROWS)
             for s in range(2):
                 high, low = split(decode(alpha_from[s], rows))
-                to = pl.ds(pl.multiple_of(s * TILE + c * ROWS, ROWS), ROWS)
+                to = pl.ds(pl.multiple_of(s * TILE + c * PROWS, PROWS), PROWS)
                 for n in range(NBLK):
                     bl[n, to, pl.ds(0, BLOCK)] = high[:, n * BLOCK : (n + 1) * BLOCK]
                     bl[n, to, pl.ds(BLOCK, BLOCK)] = low[:, n * BLOCK : (n + 1) * BLOCK]
             return 0
 
-        lax.fori_loop(0, CHUNKS, body, 0)
+        lax.fori_loop(0, PARTS, body, 0)
 
     def alpha_product(first, last):
         def body(i, _):
@@ -255,77 +255,86 @@
 
         lax.fori_loop(2 * first, 2 * last, body, 0)
 
-    def beta_product(c):
+    def beta_product(p):
         for s in range(2):
-            high, low = split(decode(beta_from[s], data_rows(c)))
-            xl[s, pl.ds(0, ROWS), :] = high
-            xl[s, pl.ds(ROWS, ROWS), :] = low
+            high, low = split(decode(beta_from[s], pl.ds(HEAD + p * PROWS, PROWS)))
+            xl[s, pl.ds(0, PROWS), :] = high
+            xl[s, pl.ds(PROWS, PROWS), :] = low
 
         part[...] = jnp.zeros_like(part)
         for s in range(2):
             for k in (pl.ds(0, 512), pl.ds(512, TILE - 512)):
                 part[...] += jnp.dot(xl[s, :, k], weights[s, k, :], preferred_element_type=F32)
-        rows = pl.ds(c * ROWS, ROWS)
-        acc[rows, :] = acc[rows, :] + (part[pl.ds(0, ROWS), :] + part[pl.ds(ROWS, ROWS), :])
-
-    def store(c):
-        rows = pl.ds(c * ROWS, ROWS)
-        return pltpu.make_async_copy(acc.at[rows, :], out_hbm.at[rows, :], store_sem.at[c])
-
-    for step in range(CHUNKS + 4):
-        if 2 <= step + 1 < CHUNKS:
-            send_z(step + 1)
-        c = step - 1
-        if 0 <= c < CHUNKS:
+        rows = pl.ds(p * PROWS, PROWS)
+        sigma = acc[rows, :] + (part[pl.ds(0, PROWS), :] + part[pl.ds(PROWS, PROWS), :])
+        gap = dv[rows, :] - energy[0]
+        acc[rows, :] = (sigma - energy[0] * cv[rows, :]) * gap / (gap * gap + 0.0625)
+
+    def store(p):
+        rows = pl.ds(p * PROWS, PROWS)
+        return pltpu.make_async_copy(acc.at[rows, :], out_hbm.at[rows, :], store_sem.at[p])
+
+    far, side = 2, 4
+    for step in range(CHUNKS + side):
+        c = step
+        if c < CHUNKS:
 
             @pl.when(inner)
             def _():
                 arrived(Z2, c)
                 pass_z(c).start()
 
-        c = step - 2
+        c = step - far
         if 0 <= c < CHUNKS:
             arrived(Z3, c)
             pass_z_far(c).start()
-        for c in (2 * step - 1, 2 * step):
-            if 0 <= c < CHUNKS:
-                arrived(X1, c)
-                pass_x(c).start()
-                arrived(Y1, c)
-                pass_y(c).start()
-        if step == 0:
+
+            @pl.when(inner)
+            def _():
+                own_to_z(c).start()
+
+        c = step - side
+        if 0 <= c < CHUNKS:
+            arrived(X1, c)
+            pass_x(c).start()
+            arrived(Y1, c)
+            pass_y(c).start()
+        if step < 2 * NBLK:
+            mask_alpha(step)
+        if step == 2:
             wrecv[0].wait_recv()
             wsend[3].start()
             wsend[4].start()
+        if step == 4:
             wrecv[1].wait_recv()
             wsend[5].start()
-        if step == 1:
+        if step == 6:
             wrecv[4].wait_recv()
             wsend[6].start()
-        if step == 4:
-            for c in range(CHUNKS):
-                arrived(X2, c)
-                arrived(Y2, c)
-            alpha_operand()
-            alpha_product(0, 3)
-            for lane in (2, 3, 5, 6):
-                wrecv[lane].wait_recv()
-        if step == 5:
-            alpha_product(3, NBLK)
-        for c in range(CHUNKS):
-            if step == max(c + 4, 5):
-                arrived(K0, c)
-
-                @pl.when(jnp.logical_not(inner))
-                def _():
-                    arrived(Z2, c)
-
-                arrived(Z4, c)
-                beta_product(c)
-                store(c).start()
 
     for c in range(CHUNKS):
-        store(c).wait()
+        arrived(X2, c)
+        arrived(Y2, c)
+    alpha_operand()
+    alpha_product(0, NBLK)
+    for lane in (2, 3, 5, 6):
+        wrecv[lane].wait_recv()
+    load_d.wait()
+    for p in range(PARTS):
+        for c in (2 * p, 2 * p + 1):
+            arrived(K0, c)
+
+            @pl.when(jnp.logical_not(inner))
+            def _():
+                arrived(Z2, c)
+
+            arrived(Z4, c)
+        beta_product(p)
+        store(p).start()
+
+    for p in range(PARTS):
+        store(p).wait()
+    for c in range(CHUNKS):
         for copy in (own_to_core(c), own_to_x(c), pass_x(c), own_to_y(c), pass_y(c), own_to_z(c), pass_z_far(c)):
             copy.wait_send()
 
@@ -342,12 +351,12 @@
     anywhere = pl.BlockSpec(memory_space=pl.ANY)
     scalars = pl.BlockSpec(memory_space=pltpu.SMEM)
     code = pltpu.VMEM((HEAD + TILE, TILE), jnp.int16)
-    sigma = pl.pallas_call(
+    return pl.pallas_call(
         kernel,
         out_shape=jax.ShapeDtypeStruct((TILE, TILE), F32),
-        in_specs=[anywhere] * 3 + [scalars] * 4,
+        in_specs=[anywhere] * 4 + [scalars] * 5,
         out_specs=anywhere,
-        scratch_shapes=[pltpu.VMEM((TILE, TILE), F32)]
+        scratch_shapes=[pltpu.VMEM((TILE, TILE), F32)] * 2
         + [code] * 9
         + [
             pltpu.VMEM((2, TILE, TILE), BF16),
@@ -355,20 +364,18 @@
             pltpu.VMEM((2, TILE, TILE), BF16),
             pltpu.VMEM((TILE, 2 * TILE), BF16),
             pltpu.VMEM((NBLK, 2 * TILE, 2 * BLOCK), BF16),
-            pltpu.VMEM((2, 2 * ROWS, TILE), BF16),
-            pltpu.VMEM((2 * ROWS, TILE), F32),
+            pltpu.VMEM((2, 2 * PROWS, TILE), BF16),
+            pltpu.VMEM((2 * PROWS, TILE), F32),
             pltpu.VMEM((TILE, TILE), F32),
-            pltpu.SemaphoreType.DMA((3,)),
+            pltpu.SemaphoreType.DMA((4,)),
             pltpu.SemaphoreType.DMA((9, CHUNKS)),
             pltpu.SemaphoreType.DMA((8, CHUNKS)),
             pltpu.SemaphoreType.DMA((7,)),
             pltpu.SemaphoreType.DMA((7,)),
-            pltpu.SemaphoreType.DMA((CHUNKS,)),
+            pltpu.SemaphoreType.DMA((PARTS,)),
         ],
         compiler_params=pltpu.CompilerParams(collective_id=0, has_side_effects=True, vmem_limit_bytes=60 * 1024 * 1024),
-    )(ci_vector, alpha_coupling, beta_coupling, alpha_mask, beta_mask, alpha_partner, beta_partner)
-    gap = diagonal - energy[0]
-    return (sigma - energy[0] * ci_vector) * gap / (gap * gap + 0.0625)
+    )(ci_vector, diagonal, alpha_coupling, beta_coupling, alpha_mask, beta_mask, alpha_partner, beta_partner, energy)
 
 
 def solution(mesh):

time: 159 us -> 132 us (0.83)
  Pallas kernels: 147 us -> 124 us
  other arithmetic: 5.41 us -> 0 us
  local copies, waits for them, and re-layouts: 2.57 us -> 6.38 us
    pallas_call x1, Pallas kernels: 147 us -> 124 us  [local(): pl.pallas_call(kernel, out_shape=jax.ShapeDtypeStruct((TILE, TILE), F32),...]
    div x1 -> x0, other arithmetic: 5.41 us -> none  [local(): return (sigma - energy[0] * ci_vector) * gap / (gap * gap + 0.0625)]
    unnamed x4 -> x3, local copies, waits for them, and re-layouts: 2.57 us -> 6.38 us
where the time goes in v2:
time: 132 us; the launch traced here: 131 us
  Pallas kernels  124 us (94%)
  local copies, waits for them, and re-layouts  6.38 us (5%)
    pallas_call x1, Pallas kernels, local(): pl.pallas_call(kernel, out_shape=jax.ShapeDtypeStruct((TILE, TILE), F32),...  124 us
    unnamed x3, local copies, waits for them, and re-layouts  6.38 us

profile of v2, /device:TPU:4, one launch (start us, length us, event | category | flops | bytes accessed | tf_op | source)
XLA Modules:
  0.0 130.6 jit_solution(2976873535088549580)
XLA Ops:
  0.7 1.3 copy.10.am
  1.9 1.3 copy.11.bm
  3.2 123.5 %shard_map.91 = f32[896,896]{1,0:T(8,128)} custom-call(f32[896,896]{1,0:T(8,128)} %ci_hbm.1, f32[896,896]{1,0:T(8,128)} %diag_hbm.1, bf16[1,2,896,896]{3,2,1,0:T(8,128)(2,1)} %ac_hbm.1, bf16[1,2,112,896]{3,2,1,0:T(8,128)(2,1)} %bc_hbm.1, s32[1,2,7,7]{3,2,1,0:T(8,128)} %copy.10.am, s32[1,2,7,7]{3,2,1,0:T(8,128)} %copy.11.bm, s32[1,2]{1,0:T(1,128)} %ap.1, ...), custom_call_target="tpu_custom_call" | custom-call | tf_op jit(solution)/shard_map/pallas_call | solution.py:354
  126.8 3.8 %copy.14 = f32[896,896]{1,0:T(8,128)} copy(f32[896,896]{1,0:T(8,128)} %shard_map.91) | data formatting | bytes 6422528

commit v3 on v2

--- a/solution.py
+++ b/solution.py
@@ -9,11 +9,11 @@
 TILE = 896
 BLOCK = 128
 NBLK = TILE // BLOCK
-HEAD = 16
 CHUNKS = 14
 ROWS = TILE // CHUNKS
 PARTS = 7
 PROWS = TILE // PARTS
+START, EARLY = 9, 4
 PIECE = 112
 LEVELS = 32767.0
 F32 = jnp.float32
@@ -23,11 +23,7 @@
 
 
 def chunk_rows(c):
-    return pl.ds(0, HEAD + ROWS) if c == 0 else pl.ds(HEAD + ROWS * c, ROWS)
-
-
-def data_rows(c):
-    return pl.ds(HEAD + ROWS * c, ROWS)
+    return pl.ds(ROWS * c, ROWS)
 
 
 def flipped(index, bit):
@@ -39,25 +35,26 @@
     return high, (value - high.astype(F32)).astype(BF16)
 
 
-def pick(choices, rows):
-    value = choices[0][1][rows, :]
-    for chosen, ref in choices[1:]:
-        value = lax.select(chosen, ref[rows, :], value)
+def pick(choices, rows, at):
+    value = choices[0][at][rows, :]
+    for choice in choices[1:]:
+        value = lax.select(choice[0], choice[at][rows, :], value)
     return value.astype(F32)
 
 
 def decode(choices, rows):
-    scale = jnp.exp2(pick(choices, pl.ds(0, HEAD)))[0:1, :]
-    root = pick(choices, rows) * (1.0 / LEVELS)
+    scale = pick(choices, pl.ds(0, 8), 2)[0:1, 0:1]
+    root = pick(choices, rows, 1) * (1.0 / LEVELS)
     return (root * jnp.abs(root)) * (root * root) * scale
 
 
 def kernel(
     ci_hbm, diag_hbm, ac_hbm, bc_hbm, am, bm, ap, bp, energy, out_hbm,
     cv, dv, own, k0, x1, x2, y1, y2, z2, z3, z4, weights, piece, ha, hat, bl, xl, part, acc,
-    load_sem, send_sem, recv_sem, wsend_sem, wrecv_sem, store_sem,
+    head, h0, h1, h2, h3, h4, h5, h6, h7, load_sem, part_sem, send_sem, recv_sem, wsend_sem, wrecv_sem, hsend_sem, hrecv_sem, store_sem,
 ):
     tiles = [k0, x1, x2, y1, y2, z2, z3, z4]
+    heads = [h0, h1, h2, h3, h4, h5, h6, h7]
     a = lax.axis_index("alpha")
     b = lax.axis_index("beta")
     y, xh = a % 4, a // 4
@@ -76,17 +73,21 @@
     sz = 1 - 2 * (t // 2)
     inner = (t == 1) | (t == 2)
 
-    load_c = pltpu.make_async_copy(ci_hbm, cv, load_sem.at[0])
+    def load_c(c):
+        rows = pl.ds(c * PROWS, PROWS)
+        return pltpu.make_async_copy(ci_hbm.at[rows, :], cv.at[rows, :], part_sem.at[c])
+
     load_p = pltpu.make_async_copy(bc_hbm.at[0], piece, load_sem.at[1])
     load_a = pltpu.make_async_copy(ac_hbm.at[0], ha, load_sem.at[2])
     load_d = pltpu.make_async_copy(diag_hbm, dv, load_sem.at[3])
-    load_c.start()
+    for c in range(PARTS):
+        load_c(c).start()
     load_p.start()
     load_a.start()
     load_d.start()
 
     barrier = pltpu.get_barrier_semaphore()
-    greet = [at(dc=1), at(dx=1), at(dx=-1), at(dx=2), at(dy=1), at(dy=-1), at(dz=1), at(dz=-1), at(dz=2), at(dz=-2)]
+    greet = [at(dc=1), at(dx=1), at(dx=-1), at(dx=2), at(dy=1), at(dy=-1), at(dy=2), at(dz=1), at(dz=-1), at(dz=2), at(dz=-2), at(dz=4)]
     for other in greet:
         pl.semaphore_signal(barrier, inc=1, device_id=other, device_id_type=MESH)
 
@@ -170,23 +171,40 @@
         wmove(1, 2, 6, at(dy=1)),
     ]
 
-    load_c.wait()
-
-    def biggest(c, value):
-        return jnp.maximum(value, jnp.max(jnp.abs(cv[pl.ds(pl.multiple_of(c * PROWS, PROWS), PROWS), :]), axis=0, keepdims=True))
-
-    column = lax.fori_loop(0, PARTS, biggest, jnp.full((1, TILE), 1e-36, F32))
+    hsend = [
+        pltpu.make_async_remote_copy(
+            src_ref=head,
+            dst_ref=heads[dst],
+            send_sem=hsend_sem.at[dst],
+            recv_sem=hrecv_sem.at[dst],
+            device_id=target,
+            device_id_type=MESH,
+        )
+        for dst, target in (
+            (K0, at(dc=1)),
+            (X1, at(dx=tx)),
+            (X2, at(dx=2)),
+            (Y1, at(dy=ty)),
+            (Y2, at(dy=2)),
+            (Z2, at(dz=tz)),
+            (Z3, at(dz=2 - 4 * ((z // 2) % 2))),
+            (Z4, at(dz=4)),
+        )
+    ]
+    column = jnp.full((1, TILE), 1e-36, F32)
+    for c in range(PARTS):
+        load_c(c).wait()
+        column = jnp.maximum(column, jnp.max(jnp.abs(cv[pl.ds(c * PROWS, PROWS), :]), axis=0, keepdims=True))
     top = jnp.max(column, axis=1, keepdims=True)
     exponent = jnp.maximum(jnp.floor(jnp.log2(top)) + 1.0, -120.0)
-    exponent = jnp.broadcast_to(exponent, (HEAD, TILE))
-    own[pl.ds(0, HEAD), :] = exponent.astype(jnp.int16)
-    shrink = jnp.exp2(-exponent[0:1, :])
+    head[...] = jnp.broadcast_to(jnp.exp2(exponent), (8, BLOCK))
+    shrink = jnp.exp2(-exponent)
 
     def encode(c):
         value = cv[pl.ds(c * ROWS, ROWS), :]
         root = jnp.sqrt(jnp.sqrt(jnp.abs(value) * shrink)) * LEVELS
         root = jnp.minimum(jnp.round(root), LEVELS)
-        own[data_rows(c), :] = jnp.where(value < 0, -root, root).astype(jnp.int16)
+        own[chunk_rows(c), :] = jnp.where(value < 0, -root, root).astype(jnp.int16)
 
     def send_z(c):
         @pl.when(inner)
@@ -213,9 +231,11 @@
             for v in range(NBLK):
                 columns = pl.ds(v * BLOCK, BLOCK)
                 block = piece[s, pl.ds(16 * k, 16), columns].astype(F32)
-                weights[s, rows, columns] = (block * bm[0, s, u, v].astype(F32)).astype(BF16)
+                weights[s, rows, columns] = (block * bm[0, u, s, v].astype(F32)).astype(BF16)
     for lane in (0, 1, 2):
         wsend[lane].start()
+    for copy in hsend:
+        copy.start()
     for c in range(CHUNKS):
         own_to_x(c).start()
         own_to_y(c).start()
@@ -226,15 +246,15 @@
     def mask_alpha(i):
         s, u = i // NBLK, i % NBLK
         for v in range(NBLK):
-            block = ha[s, pl.ds(u * BLOCK, BLOCK), pl.ds(v * BLOCK, BLOCK)].astype(F32) * am[0, s, u, v].astype(F32)
+            block = ha[s, pl.ds(u * BLOCK, BLOCK), pl.ds(v * BLOCK, BLOCK)].astype(F32) * am[0, u, s, v].astype(F32)
             hat[pl.ds(v * BLOCK, BLOCK), pl.ds(s * TILE + u * BLOCK, BLOCK)] = block.T.astype(BF16)
 
-    alpha_from = [[(ap[0, s] == flipped(a, bit), ref) for bit, ref in ((1, y1), (2, y2), (4, x2))] for s in range(2)]
-    beta_from = [[(bp[0, s] == flipped(b, bit), ref) for bit, ref in ((1, k0), (2, x1), (4, z2), (8, z3), (16, z4))] for s in range(2)]
+    alpha_from = [[(ap[0, s] == flipped(a, bit), tiles[t], heads[t]) for bit, t in ((1, Y1), (2, Y2), (4, X2))] for s in range(2)]
+    beta_from = [[(bp[0, s] == flipped(b, bit), tiles[t], heads[t]) for bit, t in ((1, K0), (2, X1), (4, Z2), (8, Z3), (16, Z4))] for s in range(2)]
 
     def alpha_operand():
         def body(c, _):
-            rows = pl.ds(pl.multiple_of(HEAD + c * PROWS, 16), PROWS)
+            rows = pl.ds(pl.multiple_of(c * PROWS, PROWS), PROWS)
             for s in range(2):
                 high, low = split(decode(alpha_from[s], rows))
                 to = pl.ds(pl.multiple_of(s * TILE + c * PROWS, PROWS), PROWS)
@@ -250,30 +270,47 @@
             n, m = i // 2, i % 2
             rows = pl.ds(pl.multiple_of(m * 448, 64), 448)
             both = jnp.dot(hat[rows, :], bl[n], preferred_element_type=F32)
-            acc[rows, pl.ds(pl.multiple_of(n * BLOCK, BLOCK), BLOCK)] = both[:, :BLOCK] + both[:, BLOCK:]
+            acc[rows, pl.ds(pl.multiple_of(n * BLOCK, BLOCK), BLOCK)] += both[:, :BLOCK] + both[:, BLOCK:]
             return 0
 
         lax.fori_loop(2 * first, 2 * last, body, 0)
 
-    def beta_product(p):
+    def beta_product(first, count):
+        rows = pl.ds(first, count)
         for s in range(2):
-            high, low = split(decode(beta_from[s], pl.ds(HEAD + p * PROWS, PROWS)))
-            xl[s, pl.ds(0, PROWS), :] = high
-            xl[s, pl.ds(PROWS, PROWS), :] = low
-
-        part[...] = jnp.zeros_like(part)
+            high, low = split(decode(beta_from[s], rows))
+            xl[s, pl.ds(0, count), :] = high
+            xl[s, pl.ds(count, count), :] = low
+
+        both = pl.ds(0, 2 * count)
         for s in range(2):
             for k in (pl.ds(0, 512), pl.ds(512, TILE - 512)):
-                part[...] += jnp.dot(xl[s, :, k], weights[s, k, :], preferred_element_type=F32)
-        rows = pl.ds(p * PROWS, PROWS)
-        sigma = acc[rows, :] + (part[pl.ds(0, PROWS), :] + part[pl.ds(PROWS, PROWS), :])
+                product = jnp.dot(xl[s, both, k], weights[s, k, :], preferred_element_type=F32)
+                if s == 0 and k.start == 0:
+                    part[both, :] = product
+                else:
+                    part[both, :] += product
+        acc[rows, :] += part[pl.ds(0, count), :] + part[pl.ds(count, count), :]
+
+    def correct(first, count):
+        rows = pl.ds(first, count)
         gap = dv[rows, :] - energy[0]
-        acc[rows, :] = (sigma - energy[0] * cv[rows, :]) * gap / (gap * gap + 0.0625)
-
-    def store(p):
-        rows = pl.ds(p * PROWS, PROWS)
-        return pltpu.make_async_copy(acc.at[rows, :], out_hbm.at[rows, :], store_sem.at[p])
-
+        acc[rows, :] = (acc[rows, :] - energy[0] * cv[rows, :]) * gap / (gap * gap + 0.0625)
+
+    def complete(c):
+        arrived(K0, c)
+
+        @pl.when(jnp.logical_not(inner))
+        def _():
+            arrived(Z2, c)
+
+        arrived(Z4, c)
+
+    def store(c):
+        rows = chunk_rows(c)
+        return pltpu.make_async_copy(acc.at[rows, :], out_hbm.at[rows, :], store_sem.at[c])
+
+    acc[...] = jnp.zeros_like(acc)
     far, side = 2, 4
     for step in range(CHUNKS + side):
         c = step
@@ -311,29 +348,39 @@
         if step == 6:
             wrecv[4].wait_recv()
             wsend[6].start()
+        if step == START:
+            for dst in range(8):
+                hsend[dst].wait_recv()
+            for lane in (2, 3, 5, 6):
+                wrecv[lane].wait_recv()
+        if step >= START and (step - START) % 2 == 0 and (step - START) // 2 < EARLY:
+            p = (step - START) // 2
+            complete(2 * p)
+            complete(2 * p + 1)
+            beta_product(p * PROWS, PROWS)
 
     for c in range(CHUNKS):
         arrived(X2, c)
         arrived(Y2, c)
     alpha_operand()
     alpha_product(0, NBLK)
-    for lane in (2, 3, 5, 6):
-        wrecv[lane].wait_recv()
     load_d.wait()
-    for p in range(PARTS):
+    for p in range(EARLY):
+        correct(p * PROWS, PROWS)
         for c in (2 * p, 2 * p + 1):
-            arrived(K0, c)
-
-            @pl.when(jnp.logical_not(inner))
-            def _():
-                arrived(Z2, c)
-
-            arrived(Z4, c)
-        beta_product(p)
-        store(p).start()
-
-    for p in range(PARTS):
-        store(p).wait()
+            store(c).start()
+    for group in [(c, c + 1) for c in range(2 * EARLY, CHUNKS - 2, 2)] + [(CHUNKS - 2,), (CHUNKS - 1,)]:
+        for c in group:
+            complete(c)
+        beta_product(group[0] * ROWS, len(group) * ROWS)
+        correct(group[0] * ROWS, len(group) * ROWS)
+        for c in group:
+            store(c).start()
+
+    for copy in hsend:
+        copy.wait_send()
+    for c in range(CHUNKS):
+        store(c).wait()
     for c in range(CHUNKS):
         for copy in (own_to_core(c), own_to_x(c), pass_x(c), own_to_y(c), pass_y(c), own_to_z(c), pass_z_far(c)):
             copy.wait_send()
@@ -348,9 +395,9 @@
 
 
 def local(ci_vector, diagonal, energy, alpha_partner, alpha_coupling, alpha_mask, beta_partner, beta_coupling, beta_mask):
-    anywhere = pl.BlockSpec(memory_space=pl.ANY)
+    anywhere = pl.BlockSpec(memory_space=pltpu.HBM)
     scalars = pl.BlockSpec(memory_space=pltpu.SMEM)
-    code = pltpu.VMEM((HEAD + TILE, TILE), jnp.int16)
+    code = pltpu.VMEM((TILE, TILE), jnp.int16)
     return pl.pallas_call(
         kernel,
         out_shape=jax.ShapeDtypeStruct((TILE, TILE), F32),
@@ -367,15 +414,21 @@
             pltpu.VMEM((2, 2 * PROWS, TILE), BF16),
             pltpu.VMEM((2 * PROWS, TILE), F32),
             pltpu.VMEM((TILE, TILE), F32),
+        ]
+        + [pltpu.VMEM((8, BLOCK), F32)] * 9
+        + [
             pltpu.SemaphoreType.DMA((4,)),
+            pltpu.SemaphoreType.DMA((PARTS,)),
             pltpu.SemaphoreType.DMA((9, CHUNKS)),
             pltpu.SemaphoreType.DMA((8, CHUNKS)),
             pltpu.SemaphoreType.DMA((7,)),
             pltpu.SemaphoreType.DMA((7,)),
-            pltpu.SemaphoreType.DMA((PARTS,)),
+            pltpu.SemaphoreType.DMA((8,)),
+            pltpu.SemaphoreType.DMA((8,)),
+            pltpu.SemaphoreType.DMA((CHUNKS,)),
         ],
-        compiler_params=pltpu.CompilerParams(collective_id=0, has_side_effects=True, vmem_limit_bytes=60 * 1024 * 1024),
-    )(ci_vector, diagonal, alpha_coupling, beta_coupling, alpha_mask, beta_mask, alpha_partner, beta_partner, energy)
+        compiler_params=pltpu.CompilerParams(collective_id=0, has_side_effects=True, vmem_limit_bytes=58 * 1024 * 1024),
+    )(ci_vector, diagonal, alpha_coupling, beta_coupling, jnp.transpose(alpha_mask, (0, 2, 1, 3)), jnp.transpose(beta_mask, (0, 2, 1, 3)), alpha_partner, beta_partner, energy)
 
 
 def solution(mesh):

time: 132 us -> 128 us (0.970)
  local copies, waits for them, and re-layouts: 6.38 us -> 3.8 us
  Pallas kernels: 124 us -> 122 us
    unnamed x3 -> x1, local copies, waits for them, and re-layouts: 6.38 us -> 3.8 us
    pallas_call x1, Pallas kernels: 124 us -> 122 us  [local(): pl.pallas_call(kernel, out_shape=jax.ShapeDtypeStruct((TILE, TILE), F32),...]
where the time goes in v3:
time: 128 us; the launch traced here: 126 us
  Pallas kernels  122 us (95%)
  local copies, waits for them, and re-layouts  3.8 us (3%)
    pallas_call x1, Pallas kernels, local(): pl.pallas_call(kernel, out_shape=jax.ShapeDtypeStruct((TILE, TILE), F32),...  122 us
    unnamed x1, local copies, waits for them, and re-layouts  3.8 us

profile of v3, /device:TPU:4, one launch (start us, length us, event | category | flops | bytes accessed | tf_op | source)
XLA Modules:
  0.0 126.2 jit_solution(18379550774031059157)
XLA Ops:
  0.7 121.7 %shard_map.91 = f32[896,896]{1,0:T(8,128)} custom-call(f32[896,896]{1,0:T(8,128)} %ci_hbm.1, f32[896,896]{1,0:T(8,128)} %diag_hbm.1, bf16[1,2,896,896]{3,2,1,0:T(8,128)(2,1)} %ac_hbm.1, bf16[1,2,112,896]{3,2,1,0:T(8,128)(2,1)} %bc_hbm.1, s32[1,7,2,7]{3,2,1,0:T(2,128)} %bitcast.2, s32[1,7,2,7]{3,2,1,0:T(2,128)} %bitcast.3, s32[1,2]{1,0:T(1,128)} %ap.1, ...), custom_call_target="tpu_custom_call" | custom-call | tf_op jit(solution)/shard_map/pallas_call | solution.py:401
  122.4 3.8 %copy.12 = f32[896,896]{1,0:T(8,128)} copy(f32[896,896]{1,0:T(8,128)} %shard_map.91) | data formatting | bytes 6422528

commit v4 on v3

--- a/solution.py
+++ b/solution.py
@@ -9,11 +9,11 @@
 TILE = 896
 BLOCK = 128
 NBLK = TILE // BLOCK
-CHUNKS = 14
+CHUNKS = 7
 ROWS = TILE // CHUNKS
 PARTS = 7
 PROWS = TILE // PARTS
-START, EARLY = 9, 4
+START, EARLY = 5, 4
 PIECE = 112
 LEVELS = 32767.0
 F32 = jnp.float32
@@ -311,7 +311,7 @@
         return pltpu.make_async_copy(acc.at[rows, :], out_hbm.at[rows, :], store_sem.at[c])
 
     acc[...] = jnp.zeros_like(acc)
-    far, side = 2, 4
+    far, side = 2, 2
     for step in range(CHUNKS + side):
         c = step
         if c < CHUNKS:
@@ -336,16 +336,17 @@
             pass_x(c).start()
             arrived(Y1, c)
             pass_y(c).start()
-        if step < 2 * NBLK:
-            mask_alpha(step)
-        if step == 2:
+        if step < NBLK:
+            mask_alpha(2 * step)
+            mask_alpha(2 * step + 1)
+        if step == 1:
             wrecv[0].wait_recv()
             wsend[3].start()
             wsend[4].start()
-        if step == 4:
+        if step == 2:
             wrecv[1].wait_recv()
             wsend[5].start()
-        if step == 6:
+        if step == 3:
             wrecv[4].wait_recv()
             wsend[6].start()
         if step == START:
@@ -353,10 +354,9 @@
                 hsend[dst].wait_recv()
             for lane in (2, 3, 5, 6):
                 wrecv[lane].wait_recv()
-        if step >= START and (step - START) % 2 == 0 and (step - START) // 2 < EARLY:
-            p = (step - START) // 2
-            complete(2 * p)
-            complete(2 * p + 1)
+        if step >= START and step - START < EARLY:
+            p = step - START
+            complete(p)
             beta_product(p * PROWS, PROWS)
 
     for c in range(CHUNKS):
@@ -367,9 +367,8 @@
     load_d.wait()
     for p in range(EARLY):
         correct(p * PROWS, PROWS)
-        for c in (2 * p, 2 * p + 1):
-            store(c).start()
-    for group in [(c, c + 1) for c in range(2 * EARLY, CHUNKS - 2, 2)] + [(CHUNKS - 2,), (CHUNKS - 1,)]:
+        store(p).start()
+    for group in [(c,) for c in range(EARLY, CHUNKS)]:
         for c in group:
             complete(c)
         beta_product(group[0] * ROWS, len(group) * ROWS)

time: 128 us -> 128 us (level)
  no operation moved by 1% of the time
where the time goes in v4:
time: 128 us; the launch traced here: 127 us
  Pallas kernels  123 us (96%)
  local copies, waits for them, and re-layouts  3.8 us (3%)
    pallas_call x1, Pallas kernels, local(): pl.pallas_call(kernel, out_shape=jax.ShapeDtypeStruct((TILE, TILE), F32),...  123 us
    unnamed x1, local copies, waits for them, and re-layouts  3.8 us

profile of v4, /device:TPU:4, one launch (start us, length us, event | category | flops | bytes accessed | tf_op | source)
XLA Modules:
  0.0 127.3 jit_solution(13007578882547784244)
XLA Ops:
  0.7 122.9 %shard_map.91 = f32[896,896]{1,0:T(8,128)} custom-call(f32[896,896]{1,0:T(8,128)} %ci_hbm.1, f32[896,896]{1,0:T(8,128)} %diag_hbm.1, bf16[1,2,896,896]{3,2,1,0:T(8,128)(2,1)} %ac_hbm.1, bf16[1,2,112,896]{3,2,1,0:T(8,128)(2,1)} %bc_hbm.1, s32[1,7,2,7]{3,2,1,0:T(2,128)} %bitcast.2, s32[1,7,2,7]{3,2,1,0:T(2,128)} %bitcast.3, s32[1,2]{1,0:T(1,128)} %ap.1, ...), custom_call_target="tpu_custom_call" | custom-call | tf_op jit(solution)/shard_map/pallas_call | solution.py:400
  123.5 3.8 %copy.12 = f32[896,896]{1,0:T(8,128)} copy(f32[896,896]{1,0:T(8,128)} %shard_map.91) | data formatting | bytes 6422528
